TPU v7x, 32 devices: a whole 2x2x4 slice. The times are simulated.
32 devices in a mesh: sub: 8 (over z, x), grp: 4 (over y, core).
Axes of the slice: x: 2, y: 2, z: 4, core: 2. Of those that a mesh axis runs over, the one named last changes fastest.
Arguments:
- rhs_field: bfloat16 [8, 4, 1024, 256], P('sub', 'grp'), may hold values from -6 to 6
- local_inverse: bfloat16 [8, 4, 1024, 1024], P('sub', 'grp'), may hold values from -0.03125 to 0.03125
- stiff_diag: float32 [8, 4, 1024], P('sub', 'grp'), may hold values from 1 to 3
- bonds: float32 [8, 4, 1024], P('sub', 'grp'), may hold values from 0.1 to 0.4
- deflation: bfloat16 [8, 4, 1024, 64], P('sub', 'grp'), as said below
- margin_rows: int32 [8, 4, 4, 128], P('sub', 'grp'), may hold values from 0 to 1023, as said below
- margin_count: int32 [8, 4, 4], P('sub', 'grp'), may hold values from 64 to 128, as said below
Outputs:
- solution: float32 [8, 4, 1024, 256], P('sub', 'grp')
- residual: bfloat16 [8, 4, 1024, 256], P('sub', 'grp')
Inputs may be any that keep to these rules, and one draw needn't show every extreme that they name: `margin_rows`: within one subdomain and direction the 128 row numbers are distinct. `margin_count`: A subdomain's count toward a neighbour equals that neighbour's count toward it in the opposite direction. `deflation`: entries have magnitude at most 6 / sqrt(1024).
All inputs are finite; a program needn't handle non-finite values.
Results may differ from a plain program's by a relative error of at most 0.0026.
Values sent between devices are 32-bit elements; how exact they have to be, the bound alone decides.
A program may use at most 64 MiB of HBM per device.

v0:
```python
import functools

import jax
import jax.numpy as jnp
from jax import lax
from jax.experimental import pallas as pl
from jax.experimental.pallas import tpu as pltpu
from jax.sharding import PartitionSpec as P

ITERS = 2
CHUNKS = 2

CHEB_FIRST = 0.4
CHEB_SECOND = 0.3
COUPLE_WEIGHT = 0.5

MESH = pl.DeviceIdType.MESH
F32 = jnp.float32
BF16 = jnp.bfloat16
NT = (((1,), (1,)), ((), ()))


def dot(a, b):
    return jnp.dot(a, b, preferred_element_type=F32)


def dot_nt(a, b):
    return lax.dot_general(a, b, NT, preferred_element_type=F32)


def pair(x):
    high = x.astype(BF16)
    low = (x - high.astype(F32)).astype(BF16)
    return jnp.concatenate([high, low], axis=1)


def fold(x):
    width = x.shape[1] // 2
    return x[:, :width] + x[:, width:]


def one_hot(hit):
    return jnp.where(hit, 1.0, 0.0).astype(BF16)


def upright(row):
    size = row.shape[1]
    return jnp.broadcast_to(row, (size, size)).T


def kernel(
    subs, groups,
    rhs_hbm, inverse_hbm, diag_row, bond_row, basis_t, rows, count,
    sol_out, res_out,
    rhs, inverse, basis, gather, scatter, cross, edge_basis, diag, inv_diag, bond_low, bond_high,
    resid, corr, total, tile, edge_out, edge_in, coarse_out, coarse_in, margin_out, margin_in,
    rhs_sem, load_sem, edge_send, edge_recv, send_sem, recv_sem,
):
    nodes, columns = rhs.shape
    defl = basis_t.shape[0]
    margin = rows.shape[1]
    width = columns // CHUNKS
    s, g = lax.axis_index("sub"), lax.axis_index("grp")
    has = [s > 0, s < subs - 1, g > 0, g < groups - 1]
    near = [(s - 1, g), (s + 1, g), (s, g - 1), (s, g + 1)]

    rhs_load = pltpu.make_async_copy(rhs_hbm, rhs, rhs_sem)
    rhs_load.start()
    load = pltpu.make_async_copy(inverse_hbm, inverse, load_sem)
    load.start()

    barrier = pltpu.get_barrier_semaphore()
    for d in range(4):
        @pl.when(has[d])
        def _(d=d):
            pl.semaphore_signal(barrier, inc=1, device_id=near[d], device_id_type=MESH)

    def edge_copy(d):
        return pltpu.make_async_remote_copy(
            src_ref=edge_out.at[d], dst_ref=edge_in.at[d ^ 1],
            send_sem=edge_send.at[d], recv_sem=edge_recv.at[d ^ 1],
            device_id=near[d], device_id_type=MESH)

    def coarse_copy(t, h, d):
        return pltpu.make_async_remote_copy(
            src_ref=coarse_out.at[t, h], dst_ref=coarse_in.at[t, h, d ^ 1],
            send_sem=send_sem.at[t, h, 2, d], recv_sem=recv_sem.at[t, h, 2, d ^ 1],
            device_id=near[d], device_id_type=MESH)

    def margin_copy(t, h, p, d):
        return pltpu.make_async_remote_copy(
            src_ref=margin_out.at[t, h, p, d], dst_ref=margin_in.at[t, h, p, d ^ 1],
            send_sem=send_sem.at[t, h, p, d], recv_sem=recv_sem.at[t, h, p, d ^ 1],
            device_id=near[d], device_id_type=MESH)

    def start(copy_to):
        for d in range(4):
            @pl.when(has[d])
            def _(d=d):
                copy_to(d).start()

    def arrive(copy_to):
        for d in range(4):
            @pl.when(has[d])
            def _(d=d):
                copy_to(d ^ 1).wait_recv()

    def sent(copy_to):
        for d in range(4):
            @pl.when(has[d])
            def _(d=d):
                copy_to(d).wait_send()

    for d in range(4):
        @pl.when(jnp.logical_not(has[d]))
        def _(d=d):
            edge_in[d] = jnp.zeros_like(edge_in[d])
            for t in range(ITERS):
                for h in range(CHUNKS):
                    coarse_in[t, h, d] = jnp.zeros_like(coarse_in[t, h, d])
                    for p in range(2):
                        margin_in[t, h, p, d] = jnp.zeros_like(margin_in[t, h, p, d])

    def cols(h):
        return pl.ds(h * width, width)

    eye = one_hot(lax.broadcasted_iota(jnp.int32, (defl, defl), 0)
                  == lax.broadcasted_iota(jnp.int32, (defl, defl), 1))
    row_values = rows[...].astype(F32)
    lane = lax.broadcasted_iota(jnp.int32, (margin, margin), 1).astype(F32)
    tall = []
    for d in range(4):
        tall.append(upright(row_values[d:d + 1]))
        for j in range(nodes // margin):
            gather[pl.ds(d * margin, margin), pl.ds(j * margin, margin)] = one_hot(tall[d] == lane + float(j * margin))

    pl.semaphore_wait(barrier, sum(h.astype(jnp.int32) for h in has))

    rhs_load.wait()
    for h in range(CHUNKS):
        coarse_out[0, h] = dot(basis_t[...], rhs[:, h * width:(h + 1) * width])
        start(functools.partial(coarse_copy, 0, h))
    edges = dot_nt(basis_t[...], gather[...])
    for d in range(4):
        edge_out[d] = edges[:, d * margin:(d + 1) * margin]
    start(edge_copy)
    basis[...] = basis_t[...].astype(F32).T.astype(BF16)

    live = []
    spot = lax.broadcasted_iota(jnp.int32, (1, margin), 1)
    for d in range(4):
        live.append(spot < jnp.where(has[d], count[d], 0))
    node = lax.broadcasted_iota(jnp.int32, (nodes, margin), 0).astype(F32)
    for d in range(4):
        target = jnp.where(live[d], row_values[d:d + 1], -1.0)
        scatter[:, d * margin:(d + 1) * margin] = one_hot(node == target)
        for e in range(4):
            cross[pl.ds(e * margin, margin), pl.ds(d * margin, margin)] = one_hot(tall[e] == target)
    for j in range(nodes // margin):
        part = pl.ds(j * margin, margin)
        tall_diag = upright(diag_row[:, j * margin:(j + 1) * margin])
        diag[part, :] = tall_diag
        inv_diag[part, :] = 1.0 / tall_diag
        bond_low[part, :] = upright(bond_row[:, j * margin:(j + 1) * margin])
    bonds = bond_low[...]
    bond_high[...] = jnp.where(node == float(nodes - 1), 0.0, pltpu.roll(bonds, nodes - 1, 0))
    bond_low[...] = jnp.where(node == 0.0, 0.0, bonds)

    def local_op(x):
        lanes = x.shape[1]
        return (diag[:, :lanes] * x - bond_low[:, :lanes] * pltpu.roll(x, 1, 0)
                - bond_high[:, :lanes] * pltpu.roll(x, nodes - 1, 0))

    edge_basis[...] = dot(gather[...], basis[...]).astype(BF16)
    pushed = local_op(basis[...].astype(F32))
    pushed_high = pushed.astype(BF16)
    pushed_low = (pushed - pushed_high.astype(F32)).astype(BF16)
    own = dot(basis_t[...], pushed_high) + dot(basis_t[...], pushed_low)

    def keep_tile(q, value):
        high = value.astype(BF16)
        tile[0, q] = high
        tile[1, q] = (value - high.astype(F32)).astype(BF16)

    keep_tile(4, (CHEB_FIRST + CHEB_SECOND) * eye.astype(F32) - CHEB_FIRST * CHEB_SECOND * own)

    def apply_tile(q, x):
        parts = pair(x)
        return fold(dot(tile[0, q], parts)) + dot(tile[1, q], parts[:, :width])

    load.wait()

    def before_coarse(t, h):
        if t == 0:
            value = rhs[:, h * width:(h + 1) * width]
            half, wide = value, value.astype(F32)
            resid[:, cols(h)] = wide
        else:
            wide = resid[:, cols(h)]
            half = wide.astype(BF16)
        value = wide * inv_diag[...] + dot(inverse[...], half)
        corr[:, cols(h)] = value
        taken = fold(dot(gather[...], pair(value)))
        for d in range(4):
            margin_out[t, h, 0, d] = taken[d * margin:(d + 1) * margin]

    for t in range(ITERS):
        seconds = []
        for h in range(CHUNKS):
            before_coarse(t, h)
        if t == 0:
            arrive(edge_copy)
            for d in range(4):
                mine = jnp.where(live[d], edge_out[d], 0.0).astype(BF16)
                keep_tile(d, (CHEB_FIRST * CHEB_SECOND * COUPLE_WEIGHT) * dot_nt(mine, edge_in[d].astype(BF16)))
        for h in range(CHUNKS):
            second = apply_tile(4, coarse_out[t, h])
            arrive(functools.partial(coarse_copy, t, h))
            for d in range(4):
                second = second + apply_tile(d, coarse_in[t, h, d])
            parts = pair(second)
            seconds.append(parts)
            taken = fold(dot(edge_basis[...], parts))
            for d in range(4):
                margin_out[t, h, 0, d] = margin_out[t, h, 0, d] + taken[d * margin:(d + 1) * margin]
            start(functools.partial(margin_copy, t, h, 0))
        for h in range(CHUNKS):
            corr[:, cols(h)] = corr[:, cols(h)] + fold(dot(basis[...], seconds[h]))
        for h in range(CHUNKS):
            arrive(functools.partial(margin_copy, t, h, 0))
            came = pair(margin_in[t, h, 0].reshape(4 * margin, width))
            taken = fold(dot(cross[...], came))
            for d in range(4):
                margin_out[t, h, 1, d] = margin_out[t, h, 0, d] + taken[d * margin:(d + 1) * margin]
            start(functools.partial(margin_copy, t, h, 1))
            summed = corr[:, cols(h)] + fold(dot(scatter[...], came))
            if t == 0:
                total[:, cols(h)] = summed
            else:
                total[:, cols(h)] = total[:, cols(h)] + summed
            if t == ITERS - 1:
                sol_out[:, cols(h)] = total[:, cols(h)]
            resid[:, cols(h)] = resid[:, cols(h)] - local_op(summed)
        for h in range(CHUNKS):
            arrive(functools.partial(margin_copy, t, h, 1))
            came = pair(margin_in[t, h, 1].reshape(4 * margin, width))
            value = resid[:, cols(h)] + COUPLE_WEIGHT * fold(dot(scatter[...], came))
            if t == ITERS - 1:
                res_out[:, cols(h)] = value.astype(BF16)
            else:
                resid[:, cols(h)] = value
                coarse_out[t + 1, h] = dot(basis_t[...], value.astype(BF16))
                start(functools.partial(coarse_copy, t + 1, h))

    sent(edge_copy)
    for t in range(ITERS):
        for h in range(CHUNKS):
            sent(functools.partial(coarse_copy, t, h))
            for p in range(2):
                sent(functools.partial(margin_copy, t, h, p))


def put_out(sol_in, res_in, sol_out, res_out, sem):
    copies = [pltpu.make_async_copy(sol_in, sol_out, sem.at[0]), pltpu.make_async_copy(res_in, res_out, sem.at[1])]
    for copy in copies:
        copy.start()
    for copy in copies:
        copy.wait()


def per_device(mesh, rhs_field, local_inverse, stiff_diag, bonds, deflation, margin_rows, margin_count):
    nodes, columns = rhs_field.shape[2:]
    defl = deflation.shape[3]
    margin = margin_rows.shape[3]
    width = columns // CHUNKS
    vmem = pl.BlockSpec(memory_space=pltpu.VMEM)
    anywhere = pl.BlockSpec(memory_space=pl.ANY)
    scratch = [
        pltpu.VMEM((nodes, columns), BF16),
        pltpu.VMEM((nodes, nodes), BF16),
        pltpu.VMEM((nodes, defl), BF16),
        pltpu.VMEM((4 * margin, nodes), BF16),
        pltpu.VMEM((nodes, 4 * margin), BF16),
        pltpu.VMEM((4 * margin, 4 * margin), BF16),
        pltpu.VMEM((4 * margin, defl), BF16),
        pltpu.VMEM((nodes, margin), F32),
        pltpu.VMEM((nodes, margin), F32),
        pltpu.VMEM((nodes, margin), F32),
        pltpu.VMEM((nodes, margin), F32),
        pltpu.VMEM((nodes, columns), F32),
        pltpu.VMEM((nodes, columns), F32),
        pltpu.VMEM((nodes, columns), F32),
        pltpu.VMEM((2, 5, defl, defl), BF16),
        pltpu.VMEM((4, defl, margin), F32),
        pltpu.VMEM((4, defl, margin), F32),
        pltpu.VMEM((ITERS, CHUNKS, defl, width), F32),
        pltpu.VMEM((ITERS, CHUNKS, 4, defl, width), F32),
        pltpu.VMEM((ITERS, CHUNKS, 2, 4, margin, width), F32),
        pltpu.VMEM((ITERS, CHUNKS, 2, 4, margin, width), F32),
        pltpu.SemaphoreType.DMA,
        pltpu.SemaphoreType.DMA,
        pltpu.SemaphoreType.DMA((4,)),
        pltpu.SemaphoreType.DMA((4,)),
        pltpu.SemaphoreType.DMA((ITERS, CHUNKS, 3, 4)),
        pltpu.SemaphoreType.DMA((ITERS, CHUNKS, 3, 4)),
    ]
    sol, res = pl.pallas_call(
        functools.partial(kernel, mesh.shape["sub"], mesh.shape["grp"]),
        out_shape=(pltpu.VMEM((nodes, columns), F32), pltpu.VMEM((nodes, columns), BF16)),
        in_specs=[anywhere, pl.BlockSpec(memory_space=pl.ANY), vmem, vmem, vmem, vmem,
                  pl.BlockSpec(memory_space=pltpu.SMEM)],
        out_specs=(vmem, vmem),
        scratch_shapes=scratch,
        compiler_params=pltpu.CompilerParams(
            collective_id=0, has_side_effects=True, vmem_limit_bytes=56 * 1024 * 1024),
    )(rhs_field[0, 0], local_inverse[0, 0], stiff_diag[0], bonds[0], jnp.swapaxes(deflation[0, 0], 0, 1), margin_rows[0, 0],
      margin_count[0, 0])
    sol, res = pl.pallas_call(
        put_out,
        out_shape=(jax.ShapeDtypeStruct((nodes, columns), F32), jax.ShapeDtypeStruct((nodes, columns), BF16)),
        in_specs=[vmem, vmem],
        out_specs=(anywhere, anywhere),
        scratch_shapes=[pltpu.SemaphoreType.DMA((2,))],
        compiler_params=pltpu.CompilerParams(vmem_limit_bytes=1024 * 1024),
    )(pltpu.with_memory_space_constraint(sol, pltpu.VMEM), pltpu.with_memory_space_constraint(res, pltpu.VMEM))
    return sol[None, None], res[None, None]


def solution(mesh):
    placed = (
        P("sub", "grp", None, None),
        P("sub", "grp", None, None),
        P("sub", "grp", None),
        P("sub", "grp", None),
        P("sub", "grp", None, None),
        P("sub", "grp", None, None),
        P("sub", "grp", None),
    )
    return jax.shard_map(
        functools.partial(per_device, mesh),
        mesh=mesh,
        in_specs=placed,
        out_specs=(P("sub", "grp", None, None), P("sub", "grp", None, None)),
        check_vma=False,
    )
```

profile of v0, /device:TPU:19, one launch (start us, length us, event | category | flops | bytes accessed | tf_op | source)
XLA Modules:
  0.0 45.4 jit_solution(5145565809160202743)
XLA Ops:
  0.6 43.6 %shard_map.86 = (f32[1024,256]{1,0:T(8,128)S(1)}, bf16[1024,256]{1,0:T(8,128)(2,1)S(1)}) custom-call(bf16[1024,256]{1,0:T(8,128)(2,1)} %bitcast.12, bf16[1024,1024]{1,0:T(8,128)(2,1)} %bitcast.11, f32[1,1024]{1,0:T(1,128)} %bitcast.14, f32[1,1024]{1,0:T(1,128)} %bitcast.15, bf16[64,1024]{1,0:T(8,128)(2,1)} %bitcast.13, s32[4,128]{1,0:T(4,128)} %bitcast.16, ...), custom_call_target="tpu_custom_call" | custom-call | tf_op jit(solution)/shard_map/pallas_call | solution.py:307
  44.3 1.2 %shard_map.87 = (f32[1024,256]{1,0:T(8,128)}, bf16[1024,256]{1,0:T(8,128)(2,1)}) custom-call(f32[1024,256]{1,0:T(8,128)S(1)} %get-tuple-element.6.sol_in, bf16[1024,256]{1,0:T(8,128)(2,1)S(1)} %get-tuple-element.7.res_in), custom_call_target="tpu_custom_call" | custom-call | tf_op jit(solution)/shard_map/pallas_call | solution.py:318
where the time goes:
time: 46 us; the launch traced here: 45.4 us
  Pallas kernels  44.8 us (97%)
  between operations  0.64 us (1%)
    pallas_call x1, Pallas kernels, per_device(): pl.pallas_call(functools.partial(kernel, mesh.shape['sub'], mesh.shape['g...  43.6 us
    pallas_call x1, Pallas kernels, per_device(): pl.pallas_call(put_out, out_shape=(jax.ShapeDtypeStruct((nodes, columns),...  1.16 us

commit v1 on v0

v1 whole, which is shorter than its diff:
```python
import functools

import jax
import jax.numpy as jnp
from jax import lax
from jax.experimental import pallas as pl
from jax.experimental.pallas import tpu as pltpu
from jax.sharding import PartitionSpec as P

ITERS = 2
CHUNKS = 2

CHEB_FIRST = 0.4
CHEB_SECOND = 0.3
COUPLE_WEIGHT = 0.5

MESH = pl.DeviceIdType.MESH
F32 = jnp.float32
BF16 = jnp.bfloat16
NT = (((1,), (1,)), ((), ()))
SUB, GRP, ALL = (0, 1), (2, 3), (0, 1, 2, 3)


def dot(a, b):
    return jnp.dot(a, b, preferred_element_type=F32)


def dot_nt(a, b):
    return lax.dot_general(a, b, NT, preferred_element_type=F32)


def pair(x):
    high = x.astype(BF16)
    low = (x - high.astype(F32)).astype(BF16)
    return jnp.concatenate([high, low], axis=1)


def fold(x):
    width = x.shape[1] // 2
    return x[:, :width] + x[:, width:]


def one_hot(hit):
    return jnp.where(hit, 1.0, 0.0).astype(BF16)


def upright(row):
    size = row.shape[1]
    return jnp.broadcast_to(row, (size, size)).T


def kernel(
    subs, groups,
    rhs_hbm, inverse_hbm, diag_row, bond_row, basis_t, rows, count,
    sol_out, res_out,
    rhs, inverse, basis, gather, scatter, cross, edge_basis, edge_cols, tiles, own_tile,
    diag, inv_diag, bond_low, bond_high,
    resid, corr, total, own_part, pulled, second, came,
    edge_out, edge_in, coarse_out, coarse_in, margin_out, margin_in,
    rhs_sem, load_sem, edge_send, edge_recv, send_sem, recv_sem,
):
    nodes, columns = rhs.shape
    defl = basis_t.shape[0]
    margin = rows.shape[1]
    width = columns // CHUNKS
    side = 2 * margin
    s, g = lax.axis_index("sub"), lax.axis_index("grp")
    has = [s > 0, s < subs - 1, g > 0, g < groups - 1]
    near = [(s - 1, g), (s + 1, g), (s, g - 1), (s, g + 1)]

    rhs_load = pltpu.make_async_copy(rhs_hbm, rhs, rhs_sem)
    rhs_load.start()

    barrier = pltpu.get_barrier_semaphore()
    for d in range(4):
        @pl.when(has[d])
        def _(d=d):
            pl.semaphore_signal(barrier, inc=1, device_id=near[d], device_id_type=MESH)

    def edge_copy(d):
        return pltpu.make_async_remote_copy(
            src_ref=edge_out.at[d], dst_ref=edge_in.at[d ^ 1],
            send_sem=edge_send.at[d], recv_sem=edge_recv.at[d ^ 1],
            device_id=near[d], device_id_type=MESH)

    def coarse_copy(t, h, d):
        return pltpu.make_async_remote_copy(
            src_ref=coarse_out.at[t, h], dst_ref=coarse_in.at[t, h, d ^ 1],
            send_sem=send_sem.at[t, h, 2, d], recv_sem=recv_sem.at[t, h, 2, d ^ 1],
            device_id=near[d], device_id_type=MESH)

    def margin_copy(t, h, p, d):
        return pltpu.make_async_remote_copy(
            src_ref=margin_out.at[t, h, p, d], dst_ref=margin_in.at[t, h, p, d ^ 1],
            send_sem=send_sem.at[t, h, p, d], recv_sem=recv_sem.at[t, h, p, d ^ 1],
            device_id=near[d], device_id_type=MESH)

    def start(copy_to, dirs=ALL):
        for d in dirs:
            @pl.when(has[d])
            def _(d=d):
                copy_to(d).start()

    def arrive(copy_to, dirs=ALL):
        for d in dirs:
            @pl.when(has[d])
            def _(d=d):
                copy_to(d ^ 1).wait_recv()

    def sent(copy_to):
        for d in range(4):
            @pl.when(has[d])
            def _(d=d):
                copy_to(d).wait_send()

    def cols(h):
        return pl.ds(h * width, width)

    def block(k):
        return pl.ds(k * side, side)

    row_values = rows[...].astype(F32)
    lane = lax.broadcasted_iota(jnp.int32, (margin, margin), 1).astype(F32)
    tall = []
    for d in range(4):
        tall.append(upright(row_values[d:d + 1]))
        for j in range(nodes // margin):
            gather[pl.ds(d * margin, margin), pl.ds(j * margin, margin)] = one_hot(tall[d] == lane + float(j * margin))
    edges = dot_nt(basis_t[...], gather[...])
    for d in range(4):
        edge_out[d] = edges[:, d * margin:(d + 1) * margin]
    rhs_load.wait()
    load = pltpu.make_async_copy(inverse_hbm, inverse, load_sem)
    load.start()
    first = dot(basis_t[...], rhs[...])
    for h in range(CHUNKS):
        coarse_out[0, h] = first[:, h * width:(h + 1) * width]

    pl.semaphore_wait(barrier, sum(h.astype(jnp.int32) for h in has))
    start(edge_copy)
    for h in range(CHUNKS):
        start(functools.partial(coarse_copy, 0, h))

    for d in range(4):
        @pl.when(jnp.logical_not(has[d]))
        def _(d=d):
            edge_in[d] = jnp.zeros_like(edge_in[d])
            for t in range(ITERS):
                for h in range(CHUNKS):
                    coarse_in[t, h, d] = jnp.zeros_like(coarse_in[t, h, d])
                    for p in range(2):
                        margin_in[t, h, p, d] = jnp.zeros_like(margin_in[t, h, p, d])

    basis[...] = basis_t[...].astype(F32).T.astype(BF16)
    edge_basis[...] = dot(gather[...], basis[...]).astype(BF16)
    for j in range(nodes // margin):
        part = pl.ds(j * margin, margin)
        tall_diag = upright(diag_row[:, j * margin:(j + 1) * margin])
        diag[part, :] = tall_diag
        inv_diag[part, :] = 1.0 / tall_diag
        bond_low[part, :] = upright(bond_row[:, j * margin:(j + 1) * margin])
    node = lax.broadcasted_iota(jnp.int32, (nodes, margin), 0).astype(F32)
    bonds = bond_low[...]
    bond_high[...] = jnp.where(node == float(nodes - 1), 0.0, pltpu.roll(bonds, nodes - 1, 0))
    bond_low[...] = jnp.where(node == 0.0, 0.0, bonds)

    def local_op(x):
        lanes = x.shape[1]
        return (diag[:, :lanes] * x - bond_low[:, :lanes] * pltpu.roll(x, 1, 0)
                - bond_high[:, :lanes] * pltpu.roll(x, nodes - 1, 0))

    def correct(t, h):
        wide = resid[:, cols(h)]
        value = corr[:, cols(h)] + wide * inv_diag[...]
        corr[:, cols(h)] = value
        taken = fold(dot(gather[...], pair(value)))
        for d in range(4):
            margin_out[t, h, 0, d] = taken[d * margin:(d + 1) * margin]

    load.wait()
    corr[...] = dot(inverse[...], rhs[...])
    for h in range(CHUNKS):
        resid[:, cols(h)] = rhs[:, h * width:(h + 1) * width].astype(F32)
        correct(0, h)

    live = []
    spot = lax.broadcasted_iota(jnp.int32, (1, margin), 1)
    for d in range(4):
        live.append(spot < jnp.where(has[d], count[d], 0))
    for d in range(4):
        target = jnp.where(live[d], row_values[d:d + 1], -1.0)
        scatter[:, d * margin:(d + 1) * margin] = one_hot(node == target)
        for e in range(4):
            cross[pl.ds(e * margin, margin), pl.ds(d * margin, margin)] = one_hot(tall[e] == target)
        edge_cols[:, d * margin:(d + 1) * margin] = jnp.where(live[d], edge_out[d], 0.0).astype(BF16)

    def keep_stacked(ref, value):
        high = value.astype(BF16)
        ref[:defl] = high
        ref[defl:] = (value - high.astype(F32)).astype(BF16)

    def apply_stacked(ref, parts):
        both = dot(ref[...], parts)
        return fold(both[:defl]) + both[defl:, :width]

    pushed = pair(local_op(basis[...].astype(F32)))
    own = fold(dot(basis_t[...], pushed))
    eye = (lax.broadcasted_iota(jnp.int32, (defl, defl), 0)
           == lax.broadcasted_iota(jnp.int32, (defl, defl), 1)).astype(F32)
    keep_stacked(own_tile, (CHEB_FIRST + CHEB_SECOND) * eye - CHEB_FIRST * CHEB_SECOND * own)
    for h in range(CHUNKS):
        own_part[h] = apply_stacked(own_tile, pair(coarse_out[0, h]))

    arrive(edge_copy)
    scale = CHEB_FIRST * CHEB_SECOND * COUPLE_WEIGHT
    keep_stacked(tiles, jnp.concatenate([
        scale * dot_nt(edge_cols[:, d * margin:(d + 1) * margin], edge_in[d].astype(BF16)) for d in range(4)], axis=1))

    def send_margin(t, h):
        arrive(functools.partial(coarse_copy, t, h), GRP)
        arrive(functools.partial(coarse_copy, t, h), SUB)
        parts = pair(own_part[h] + apply_stacked(tiles, pair(coarse_in[t, h].reshape(4 * defl, width))))
        second[h] = parts
        for k, dirs in enumerate((SUB, GRP)):
            taken = fold(dot(edge_basis[block(k), :], parts))
            for d in dirs:
                margin_out[t, h, 0, d] = margin_out[t, h, 0, d] + taken[(d % 2) * margin:(d % 2 + 1) * margin]
            start(functools.partial(margin_copy, t, h, 0), dirs)

    def lift(h):
        corr[:, cols(h)] = corr[:, cols(h)] + fold(dot(basis[...], second[h]))

    def take(t, h, p, k):
        arrive(functools.partial(margin_copy, t, h, p), (SUB, GRP)[k])
        parts = pair(margin_in[t, h, p, 2 * k:2 * k + 2].reshape(side, width))
        came[h, block(k), :] = parts
        return parts

    def send_summed(t, h):
        taken = fold(dot(cross[:, side:], take(t, h, 0, 1)))
        for d in range(4):
            margin_out[t, h, 1, d] = margin_out[t, h, 0, d] + taken[d * margin:(d + 1) * margin]
        parts = take(t, h, 0, 0)
        for k, dirs in enumerate((SUB, GRP)):
            taken = fold(dot(cross[block(k), :side], parts))
            for d in dirs:
                margin_out[t, h, 1, d] = margin_out[t, h, 1, d] + taken[(d % 2) * margin:(d % 2 + 1) * margin]
            start(functools.partial(margin_copy, t, h, 1), dirs)

    def add_up(t, h):
        summed = corr[:, cols(h)] + fold(dot(scatter[...], came[h]))
        if t == 0:
            total[:, cols(h)] = summed
        else:
            total[:, cols(h)] = total[:, cols(h)] + summed
        if t == ITERS - 1:
            sol_out[:, cols(h)] = total[:, cols(h)]
        value = resid[:, cols(h)] - local_op(summed)
        resid[:, cols(h)] = value
        if t < ITERS - 1:
            pulled[h] = fold(dot(basis_t[...], pair(value)))

    def send_coarse(t, h):
        take(t, h, 1, 1)
        take(t, h, 1, 0)
        value = pulled[h] + COUPLE_WEIGHT * fold(dot(edge_cols[...], came[h]))
        coarse_out[t + 1, h] = value
        start(functools.partial(coarse_copy, t + 1, h))

    def renew(t, h):
        own_part[h] = apply_stacked(own_tile, pair(coarse_out[t, h]))
        value = resid[:, cols(h)] + COUPLE_WEIGHT * fold(dot(scatter[...], came[h]))
        resid[:, cols(h)] = value
        corr[:, cols(h)] = dot(inverse[...], value.astype(BF16))
        correct(t, h)

    for t in range(ITERS):
        for h in range(CHUNKS):
            send_margin(t, h)
            if t > 0 and h == 0:
                renew(t, CHUNKS - 1)
            lift(h)
        for h in range(CHUNKS):
            send_summed(t, h)
            add_up(t, h)
        for h in range(CHUNKS):
            if t < ITERS - 1:
                send_coarse(t, h)
                if h < CHUNKS - 1:
                    renew(t + 1, h)
            else:
                parts = take(t, h, 1, 1)
                resid[:, cols(h)] = resid[:, cols(h)] + COUPLE_WEIGHT * fold(dot(scatter[:, side:], parts))
                parts = take(t, h, 1, 0)
                res_out[:, cols(h)] = (
                    resid[:, cols(h)] + COUPLE_WEIGHT * fold(dot(scatter[:, :side], parts))).astype(BF16)

    sent(edge_copy)
    for t in range(ITERS):
        for h in range(CHUNKS):
            sent(functools.partial(coarse_copy, t, h))
            for p in range(2):
                sent(functools.partial(margin_copy, t, h, p))


def put_out(sol_in, res_in, sol_out, res_out, sem):
    copies = [pltpu.make_async_copy(sol_in, sol_out, sem.at[0]), pltpu.make_async_copy(res_in, res_out, sem.at[1])]
    for copy in copies:
        copy.start()
    for copy in copies:
        copy.wait()


def per_device(mesh, rhs_field, local_inverse, stiff_diag, bonds, deflation, margin_rows, margin_count):
    nodes, columns = rhs_field.shape[2:]
    defl = deflation.shape[3]
    margin = margin_rows.shape[3]
    width = columns // CHUNKS
    vmem = pl.BlockSpec(memory_space=pltpu.VMEM)
    anywhere = pl.BlockSpec(memory_space=pl.ANY)
    scratch = [
        pltpu.VMEM((nodes, columns), BF16),
        pltpu.VMEM((nodes, nodes), BF16),
        pltpu.VMEM((nodes, defl), BF16),
        pltpu.VMEM((4 * margin, nodes), BF16),
        pltpu.VMEM((nodes, 4 * margin), BF16),
        pltpu.VMEM((4 * margin, 4 * margin), BF16),
        pltpu.VMEM((4 * margin, defl), BF16),
        pltpu.VMEM((defl, 4 * margin), BF16),
        pltpu.VMEM((2 * defl, 4 * defl), BF16),
        pltpu.VMEM((2 * defl, defl), BF16),
        pltpu.VMEM((nodes, margin), F32),
        pltpu.VMEM((nodes, margin), F32),
        pltpu.VMEM((nodes, margin), F32),
        pltpu.VMEM((nodes, margin), F32),
        pltpu.VMEM((nodes, columns), F32),
        pltpu.VMEM((nodes, columns), F32),
        pltpu.VMEM((nodes, columns), F32),
        pltpu.VMEM((CHUNKS, defl, width), F32),
        pltpu.VMEM((CHUNKS, defl, width), F32),
        pltpu.VMEM((CHUNKS, defl, 2 * width), BF16),
        pltpu.VMEM((CHUNKS, 4 * margin, 2 * width), BF16),
        pltpu.VMEM((4, defl, margin), F32),
        pltpu.VMEM((4, defl, margin), F32),
        pltpu.VMEM((ITERS, CHUNKS, defl, width), F32),
        pltpu.VMEM((ITERS, CHUNKS, 4, defl, width), F32),
        pltpu.VMEM((ITERS, CHUNKS, 2, 4, margin, width), F32),
        pltpu.VMEM((ITERS, CHUNKS, 2, 4, margin, width), F32),
        pltpu.SemaphoreType.DMA,
        pltpu.SemaphoreType.DMA,
        pltpu.SemaphoreType.DMA((4,)),
        pltpu.SemaphoreType.DMA((4,)),
        pltpu.SemaphoreType.DMA((ITERS, CHUNKS, 3, 4)),
        pltpu.SemaphoreType.DMA((ITERS, CHUNKS, 3, 4)),
    ]
    sol, res = pl.pallas_call(
        functools.partial(kernel, mesh.shape["sub"], mesh.shape["grp"]),
        out_shape=(pltpu.VMEM((nodes, columns), F32), pltpu.VMEM((nodes, columns), BF16)),
        in_specs=[anywhere, pl.BlockSpec(memory_space=pl.ANY), vmem, vmem, vmem, vmem,
                  pl.BlockSpec(memory_space=pltpu.SMEM)],
        out_specs=(vmem, vmem),
        scratch_shapes=scratch,
        compiler_params=pltpu.CompilerParams(
            collective_id=0, has_side_effects=True, vmem_limit_bytes=56 * 1024 * 1024),
    )(rhs_field[0, 0], local_inverse[0, 0], stiff_diag[0], bonds[0], jnp.swapaxes(deflation[0, 0], 0, 1), margin_rows[0, 0],
      margin_count[0, 0])
    sol, res = pl.pallas_call(
        put_out,
        out_shape=(jax.ShapeDtypeStruct((nodes, columns), F32), jax.ShapeDtypeStruct((nodes, columns), BF16)),
        in_specs=[vmem, vmem],
        out_specs=(anywhere, anywhere),
        scratch_shapes=[pltpu.SemaphoreType.DMA((2,))],
        compiler_params=pltpu.CompilerParams(vmem_limit_bytes=1024 * 1024),
    )(pltpu.with_memory_space_constraint(sol, pltpu.VMEM), pltpu.with_memory_space_constraint(res, pltpu.VMEM))
    return sol[None, None], res[None, None]


def solution(mesh):
    placed = (
        P("sub", "grp", None, None),
        P("sub", "grp", None, None),
        P("sub", "grp", None),
        P("sub", "grp", None),
        P("sub", "grp", None, None),
        P("sub", "grp", None, None),
        P("sub", "grp", None),
    )
    return jax.shard_map(
        functools.partial(per_device, mesh),
        mesh=mesh,
        in_specs=placed,
        out_specs=(P("sub", "grp", None, None), P("sub", "grp", None, None)),
        check_vma=False,
    )
```

time: 46 us -> 42.2 us (0.917)
  Pallas kernels: 44.8 us -> 41 us
    pallas_call x1, Pallas kernels: 43.6 us -> 39.9 us  [per_device(): pl.pallas_call(functools.partial(kernel, mesh.shape['sub'], mesh.shape['g...]
where the time goes in v1:
time: 42.2 us; the launch traced here: 41.7 us
  Pallas kernels  41 us (97%)
  between operations  0.64 us (2%)
    pallas_call x1, Pallas kernels, per_device(): pl.pallas_call(functools.partial(kernel, mesh.shape['sub'], mesh.shape['g...  39.9 us
    pallas_call x1, Pallas kernels, per_device(): pl.pallas_call(put_out, out_shape=(jax.ShapeDtypeStruct((nodes, columns),...  1.16 us

profile of v1, /device:TPU:19, one launch (start us, length us, event | category | flops | bytes accessed | tf_op | source)
XLA Modules:
  0.0 41.7 jit_solution(2456020602541892064)
XLA Ops:
  0.6 39.9 %shard_map.86 = (f32[1024,256]{1,0:T(8,128)S(1)}, bf16[1024,256]{1,0:T(8,128)(2,1)S(1)}) custom-call(bf16[1024,256]{1,0:T(8,128)(2,1)} %bitcast.12, bf16[1024,1024]{1,0:T(8,128)(2,1)} %bitcast.11, f32[1,1024]{1,0:T(1,128)} %bitcast.14, f32[1,1024]{1,0:T(1,128)} %bitcast.15, bf16[64,1024]{1,0:T(8,128)(2,1)} %bitcast.13, s32[4,128]{1,0:T(4,128)} %bitcast.16, ...), custom_call_target="tpu_custom_call" | custom-call | tf_op jit(solution)/shard_map/pallas_call | solution.py:356
  40.5 1.2 %shard_map.87 = (f32[1024,256]{1,0:T(8,128)}, bf16[1024,256]{1,0:T(8,128)(2,1)}) custom-call(f32[1024,256]{1,0:T(8,128)S(1)} %get-tuple-element.6.sol_in, bf16[1024,256]{1,0:T(8,128)(2,1)S(1)} %get-tuple-element.7.res_in), custom_call_target="tpu_custom_call" | custom-call | tf_op jit(solution)/shard_map/pallas_call | solution.py:367

commit v2 on v1

--- a/solution.py
+++ b/solution.py
@@ -52,12 +52,12 @@
 def kernel(
     subs, groups,
     rhs_hbm, inverse_hbm, diag_row, bond_row, basis_t, rows, count,
-    sol_out, res_out,
-    rhs, inverse, basis, gather, scatter, cross, edge_basis, edge_cols, tiles, own_tile,
+    sol_out, head_out, tail_out, spread, parts_out,
+    rhs, inverse, gather, cross, edge_basis, edge_cols, tiles, own_tile,
     diag, inv_diag, bond_low, bond_high,
-    resid, corr, total, own_part, pulled, second, came,
+    resid, corr, total, own_part, pulled, came,
     edge_out, edge_in, coarse_out, coarse_in, margin_out, margin_in,
-    rhs_sem, load_sem, edge_send, edge_recv, send_sem, recv_sem,
+    edge_recv, send_sem, recv_sem,
 ):
     nodes, columns = rhs.shape
     defl = basis_t.shape[0]
@@ -68,7 +68,7 @@
     has = [s > 0, s < subs - 1, g > 0, g < groups - 1]
     near = [(s - 1, g), (s + 1, g), (s, g - 1), (s, g + 1)]
 
-    rhs_load = pltpu.make_async_copy(rhs_hbm, rhs, rhs_sem)
+    rhs_load = pltpu.make_async_copy(rhs_hbm, rhs, send_sem.at[1, 1, 0])
     rhs_load.start()
 
     barrier = pltpu.get_barrier_semaphore()
@@ -80,20 +80,25 @@
     def edge_copy(d):
         return pltpu.make_async_remote_copy(
             src_ref=edge_out.at[d], dst_ref=edge_in.at[d ^ 1],
-            send_sem=edge_send.at[d], recv_sem=edge_recv.at[d ^ 1],
+            send_sem=send_sem.at[0, 1, d], recv_sem=edge_recv.at[d ^ 1],
             device_id=near[d], device_id_type=MESH)
 
     def coarse_copy(t, h, d):
         return pltpu.make_async_remote_copy(
             src_ref=coarse_out.at[t, h], dst_ref=coarse_in.at[t, h, d ^ 1],
-            send_sem=send_sem.at[t, h, 2, d], recv_sem=recv_sem.at[t, h, 2, d ^ 1],
+            send_sem=send_sem.at[h, 3 * t % 2, d], recv_sem=recv_sem.at[h, 3 * t % 2, d ^ 1],
             device_id=near[d], device_id_type=MESH)
 
     def margin_copy(t, h, p, d):
         return pltpu.make_async_remote_copy(
             src_ref=margin_out.at[t, h, p, d], dst_ref=margin_in.at[t, h, p, d ^ 1],
-            send_sem=send_sem.at[t, h, p, d], recv_sem=recv_sem.at[t, h, p, d ^ 1],
+            send_sem=send_sem.at[h, (3 * t + 1 + p) % 2, d], recv_sem=recv_sem.at[h, (3 * t + 1 + p) % 2, d ^ 1],
             device_id=near[d], device_id_type=MESH)
+
+    def step_copy(k, h):
+        if k % 3 == 0:
+            return functools.partial(coarse_copy, k // 3, h)
+        return functools.partial(margin_copy, k // 3, h, k % 3 - 1)
 
     def start(copy_to, dirs=ALL):
         for d in dirs:
@@ -101,6 +106,14 @@
             def _(d=d):
                 copy_to(d).start()
 
+    def send(k, h, dirs=ALL):
+        for d in dirs:
+            @pl.when(has[d])
+            def _(d=d):
+                if k >= 2:
+                    step_copy(k - 2, h)(d).wait_send()
+                step_copy(k, h)(d).start()
+
     def arrive(copy_to, dirs=ALL):
         for d in dirs:
             @pl.when(has[d])
@@ -113,6 +126,8 @@
             def _(d=d):
                 copy_to(d).wait_send()
 
+    scatter, basis = spread.at[:, :4 * margin], spread.at[:, 4 * margin:]
+
     def cols(h):
         return pl.ds(h * width, width)
 
@@ -130,7 +145,7 @@
     for d in range(4):
         edge_out[d] = edges[:, d * margin:(d + 1) * margin]
     rhs_load.wait()
-    load = pltpu.make_async_copy(inverse_hbm, inverse, load_sem)
+    load = pltpu.make_async_copy(inverse_hbm, inverse, send_sem.at[1, 1, 1])
     load.start()
     first = dot(basis_t[...], rhs[...])
     for h in range(CHUNKS):
@@ -139,7 +154,7 @@
     pl.semaphore_wait(barrier, sum(h.astype(jnp.int32) for h in has))
     start(edge_copy)
     for h in range(CHUNKS):
-        start(functools.partial(coarse_copy, 0, h))
+        send(0, h)
 
     for d in range(4):
         @pl.when(jnp.logical_not(has[d]))
@@ -181,7 +196,7 @@
     corr[...] = dot(inverse[...], rhs[...])
     for h in range(CHUNKS):
         resid[:, cols(h)] = rhs[:, h * width:(h + 1) * width].astype(F32)
-        correct(0, h)
+    correct(0, 0)
 
     live = []
     spot = lax.broadcasted_iota(jnp.int32, (1, margin), 1)
@@ -212,6 +227,7 @@
         own_part[h] = apply_stacked(own_tile, pair(coarse_out[0, h]))
 
     arrive(edge_copy)
+    sent(edge_copy)
     scale = CHEB_FIRST * CHEB_SECOND * COUPLE_WEIGHT
     keep_stacked(tiles, jnp.concatenate([
         scale * dot_nt(edge_cols[:, d * margin:(d + 1) * margin], edge_in[d].astype(BF16)) for d in range(4)], axis=1))
@@ -220,15 +236,12 @@
         arrive(functools.partial(coarse_copy, t, h), GRP)
         arrive(functools.partial(coarse_copy, t, h), SUB)
         parts = pair(own_part[h] + apply_stacked(tiles, pair(coarse_in[t, h].reshape(4 * defl, width))))
-        second[h] = parts
+        came[h, 4 * margin:, :] = parts
         for k, dirs in enumerate((SUB, GRP)):
             taken = fold(dot(edge_basis[block(k), :], parts))
             for d in dirs:
                 margin_out[t, h, 0, d] = margin_out[t, h, 0, d] + taken[(d % 2) * margin:(d % 2 + 1) * margin]
-            start(functools.partial(margin_copy, t, h, 0), dirs)
-
-    def lift(h):
-        corr[:, cols(h)] = corr[:, cols(h)] + fold(dot(basis[...], second[h]))
+            send(3 * t + 1, h, dirs)
 
     def take(t, h, p, k):
         arrive(functools.partial(margin_copy, t, h, p), (SUB, GRP)[k])
@@ -245,10 +258,10 @@
             taken = fold(dot(cross[block(k), :side], parts))
             for d in dirs:
                 margin_out[t, h, 1, d] = margin_out[t, h, 1, d] + taken[(d % 2) * margin:(d % 2 + 1) * margin]
-            start(functools.partial(margin_copy, t, h, 1), dirs)
+            send(3 * t + 2, h, dirs)
 
     def add_up(t, h):
-        summed = corr[:, cols(h)] + fold(dot(scatter[...], came[h]))
+        summed = corr[:, cols(h)] + fold(dot(spread[...], came[h]))
         if t == 0:
             total[:, cols(h)] = summed
         else:
@@ -263,13 +276,13 @@
     def send_coarse(t, h):
         take(t, h, 1, 1)
         take(t, h, 1, 0)
-        value = pulled[h] + COUPLE_WEIGHT * fold(dot(edge_cols[...], came[h]))
+        value = pulled[h] + COUPLE_WEIGHT * fold(dot(edge_cols[...], came[h, :4 * margin]))
         coarse_out[t + 1, h] = value
-        start(functools.partial(coarse_copy, t + 1, h))
+        send(3 * t + 3, h)
 
     def renew(t, h):
         own_part[h] = apply_stacked(own_tile, pair(coarse_out[t, h]))
-        value = resid[:, cols(h)] + COUPLE_WEIGHT * fold(dot(scatter[...], came[h]))
+        value = resid[:, cols(h)] + COUPLE_WEIGHT * fold(dot(scatter[...], came[h, :4 * margin]))
         resid[:, cols(h)] = value
         corr[:, cols(h)] = dot(inverse[...], value.astype(BF16))
         correct(t, h)
@@ -277,9 +290,10 @@
     for t in range(ITERS):
         for h in range(CHUNKS):
             send_margin(t, h)
+            if t == 0 and h < CHUNKS - 1:
+                correct(0, h + 1)
             if t > 0 and h == 0:
                 renew(t, CHUNKS - 1)
-            lift(h)
         for h in range(CHUNKS):
             send_summed(t, h)
             add_up(t, h)
@@ -290,23 +304,34 @@
                     renew(t + 1, h)
             else:
                 parts = take(t, h, 1, 1)
-                resid[:, cols(h)] = resid[:, cols(h)] + COUPLE_WEIGHT * fold(dot(scatter[:, side:], parts))
+                value = resid[:, cols(h)] + COUPLE_WEIGHT * fold(dot(scatter[:, side:], parts))
+                if h < CHUNKS - 1:
+                    resid[:, cols(h)] = value
+                else:
+                    tail_out[...] = value
                 parts = take(t, h, 1, 0)
-                res_out[:, cols(h)] = (
-                    resid[:, cols(h)] + COUPLE_WEIGHT * fold(dot(scatter[:, :side], parts))).astype(BF16)
-
-    sent(edge_copy)
-    for t in range(ITERS):
-        for h in range(CHUNKS):
-            sent(functools.partial(coarse_copy, t, h))
-            for p in range(2):
-                sent(functools.partial(margin_copy, t, h, p))
-
-
-def put_out(sol_in, res_in, sol_out, res_out, sem):
-    copies = [pltpu.make_async_copy(sol_in, sol_out, sem.at[0]), pltpu.make_async_copy(res_in, res_out, sem.at[1])]
-    for copy in copies:
-        copy.start()
+                if h < CHUNKS - 1:
+                    head_out[:, cols(h)] = (
+                        resid[:, cols(h)] + COUPLE_WEIGHT * fold(dot(scatter[:, :side], parts))).astype(BF16)
+                else:
+                    parts_out[...] = parts
+
+    for h in range(CHUNKS):
+        for k in (3 * ITERS - 2, 3 * ITERS - 1):
+            sent(step_copy(k, h))
+
+
+def put_out(sol_in, head, tail, spread, parts, sol_out, res_out, last, sem):
+    rest = head.shape[1]
+    copies = [
+        pltpu.make_async_copy(sol_in, sol_out, sem.at[0]),
+        pltpu.make_async_copy(head, res_out.at[:, pl.ds(0, rest)], sem.at[1]),
+        pltpu.make_async_copy(last, res_out.at[:, pl.ds(rest, last.shape[1])], sem.at[2]),
+    ]
+    copies[0].start()
+    copies[1].start()
+    last[...] = (tail[...] + COUPLE_WEIGHT * fold(dot(spread[:, :parts.shape[0]], parts[...]))).astype(BF16)
+    copies[2].start()
     for copy in copies:
         copy.wait()
 
@@ -321,9 +346,7 @@
     scratch = [
         pltpu.VMEM((nodes, columns), BF16),
         pltpu.VMEM((nodes, nodes), BF16),
-        pltpu.VMEM((nodes, defl), BF16),
         pltpu.VMEM((4 * margin, nodes), BF16),
-        pltpu.VMEM((nodes, 4 * margin), BF16),
         pltpu.VMEM((4 * margin, 4 * margin), BF16),
         pltpu.VMEM((4 * margin, defl), BF16),
         pltpu.VMEM((defl, 4 * margin), BF16),
@@ -338,40 +361,43 @@
         pltpu.VMEM((nodes, columns), F32),
         pltpu.VMEM((CHUNKS, defl, width), F32),
         pltpu.VMEM((CHUNKS, defl, width), F32),
-        pltpu.VMEM((CHUNKS, defl, 2 * width), BF16),
-        pltpu.VMEM((CHUNKS, 4 * margin, 2 * width), BF16),
+        pltpu.VMEM((CHUNKS, 4 * margin + defl, 2 * width), BF16),
         pltpu.VMEM((4, defl, margin), F32),
         pltpu.VMEM((4, defl, margin), F32),
         pltpu.VMEM((ITERS, CHUNKS, defl, width), F32),
         pltpu.VMEM((ITERS, CHUNKS, 4, defl, width), F32),
         pltpu.VMEM((ITERS, CHUNKS, 2, 4, margin, width), F32),
         pltpu.VMEM((ITERS, CHUNKS, 2, 4, margin, width), F32),
-        pltpu.SemaphoreType.DMA,
-        pltpu.SemaphoreType.DMA,
         pltpu.SemaphoreType.DMA((4,)),
-        pltpu.SemaphoreType.DMA((4,)),
-        pltpu.SemaphoreType.DMA((ITERS, CHUNKS, 3, 4)),
-        pltpu.SemaphoreType.DMA((ITERS, CHUNKS, 3, 4)),
+        pltpu.SemaphoreType.DMA((CHUNKS, 2, 4)),
+        pltpu.SemaphoreType.DMA((CHUNKS, 2, 4)),
     ]
-    sol, res = pl.pallas_call(
+    results = (
+        pltpu.VMEM((nodes, columns), F32),
+        pltpu.VMEM((nodes, columns - width), BF16),
+        pltpu.VMEM((nodes, width), F32),
+        pltpu.VMEM((nodes, 4 * margin + defl), BF16),
+        pltpu.VMEM((2 * margin, 2 * width), BF16),
+    )
+    held = pl.pallas_call(
         functools.partial(kernel, mesh.shape["sub"], mesh.shape["grp"]),
-        out_shape=(pltpu.VMEM((nodes, columns), F32), pltpu.VMEM((nodes, columns), BF16)),
+        out_shape=results,
         in_specs=[anywhere, pl.BlockSpec(memory_space=pl.ANY), vmem, vmem, vmem, vmem,
                   pl.BlockSpec(memory_space=pltpu.SMEM)],
-        out_specs=(vmem, vmem),
+        out_specs=(vmem,) * len(results),
         scratch_shapes=scratch,
         compiler_params=pltpu.CompilerParams(
-            collective_id=0, has_side_effects=True, vmem_limit_bytes=56 * 1024 * 1024),
+            collective_id=0, has_side_effects=True, vmem_limit_bytes=60 * 1024 * 1024),
     )(rhs_field[0, 0], local_inverse[0, 0], stiff_diag[0], bonds[0], jnp.swapaxes(deflation[0, 0], 0, 1), margin_rows[0, 0],
       margin_count[0, 0])
     sol, res = pl.pallas_call(
         put_out,
         out_shape=(jax.ShapeDtypeStruct((nodes, columns), F32), jax.ShapeDtypeStruct((nodes, columns), BF16)),
-        in_specs=[vmem, vmem],
+        in_specs=[vmem] * len(results),
         out_specs=(anywhere, anywhere),
-        scratch_shapes=[pltpu.SemaphoreType.DMA((2,))],
-        compiler_params=pltpu.CompilerParams(vmem_limit_bytes=1024 * 1024),
-    )(pltpu.with_memory_space_constraint(sol, pltpu.VMEM), pltpu.with_memory_space_constraint(res, pltpu.VMEM))
+        scratch_shapes=[pltpu.VMEM((nodes, width), BF16), pltpu.SemaphoreType.DMA((3,))],
+        compiler_params=pltpu.CompilerParams(vmem_limit_bytes=8 * 1024 * 1024),
+    )(*[pltpu.with_memory_space_constraint(x, pltpu.VMEM) for x in held])
     return sol[None, None], res[None, None]
 
 

time: 42.2 us -> 41.2 us (0.976)
  Pallas kernels: 41 us -> 40.3 us
    pallas_call x1, Pallas kernels: 39.9 us -> 39.2 us  [per_device(): pl.pallas_call(functools.partial(kernel, mesh.shape['sub'], mesh.shape['g...]
where the time goes in v2:
time: 41.2 us; the launch traced here: 41 us
  Pallas kernels  40.3 us (98%)
  between operations  0.64 us (2%)
    pallas_call x1, Pallas kernels, per_device(): pl.pallas_call(functools.partial(kernel, mesh.shape['sub'], mesh.shape['g...  39.2 us
    pallas_call x1, Pallas kernels, per_device(): pl.pallas_call(put_out, out_shape=(jax.ShapeDtypeStruct((nodes, columns),...  1.18 us

profile of v2, /device:TPU:19, one launch (start us, length us, event | category | flops | bytes accessed | tf_op | source)
XLA Modules:
  0.0 41.0 jit_solution(14528085695368879084)
XLA Ops:
  0.6 39.2 %shard_map.86 = (f32[1024,256]{1,0:T(8,128)S(1)}, bf16[1024,128]{1,0:T(8,128)(2,1)S(1)}, f32[1024,128]{1,0:T(8,128)S(1)}, bf16[1024,576]{1,0:T(8,128)(2,1)S(1)}, bf16[256,256]{1,0:T(8,128)(2,1)S(1)}) custom-call(bf16[1024,256]{1,0:T(8,128)(2,1)} %bitcast.12, bf16[1024,1024]{1,0:T(8,128)(2,1)} %bitcast.11, f32[1,1024]{1,0:T(1,128)} %bitcast.14, ...), custom_call_target="tpu_custom_call" | custom-call | tf_op jit(solution)/shard_map/pallas_call | solution.py:382
  39.8 1.2 %shard_map.87 = (f32[1024,256]{1,0:T(8,128)}, bf16[1024,256]{1,0:T(8,128)(2,1)}) custom-call(f32[1024,256]{1,0:T(8,128)S(1)} %get-tuple-element.9.sol_in, bf16[1024,128]{1,0:T(8,128)(2,1)S(1)} %get-tuple-element.10.head, f32[1024,128]{1,0:T(8,128)S(1)} %get-tuple-element.11.tail, bf16[1024,576]{1,0:T(8,128)(2,1)S(1)} %get-tuple-element.12.spread, ...), custom_call_target="tpu_custom_call" | custom-call | tf_op jit(solution)/shard_map/pallas_call | solution.py:393

commit v3 on v2

--- a/solution.py
+++ b/solution.py
@@ -86,13 +86,13 @@
     def coarse_copy(t, h, d):
         return pltpu.make_async_remote_copy(
             src_ref=coarse_out.at[t, h], dst_ref=coarse_in.at[t, h, d ^ 1],
-            send_sem=send_sem.at[h, 3 * t % 2, d], recv_sem=recv_sem.at[h, 3 * t % 2, d ^ 1],
+            send_sem=send_sem.at[h, 0, d], recv_sem=recv_sem.at[h, 3 * t % 2, d ^ 1],
             device_id=near[d], device_id_type=MESH)
 
     def margin_copy(t, h, p, d):
         return pltpu.make_async_remote_copy(
             src_ref=margin_out.at[t, h, p, d], dst_ref=margin_in.at[t, h, p, d ^ 1],
-            send_sem=send_sem.at[h, (3 * t + 1 + p) % 2, d], recv_sem=recv_sem.at[h, (3 * t + 1 + p) % 2, d ^ 1],
+            send_sem=send_sem.at[h, 0, d], recv_sem=recv_sem.at[h, (3 * t + 1 + p) % 2, d ^ 1],
             device_id=near[d], device_id_type=MESH)
 
     def step_copy(k, h):
@@ -110,8 +110,8 @@
         for d in dirs:
             @pl.when(has[d])
             def _(d=d):
-                if k >= 2:
-                    step_copy(k - 2, h)(d).wait_send()
+                if k >= 1:
+                    step_copy(k - 1, h)(d).wait_send()
                 step_copy(k, h)(d).start()
 
     def arrive(copy_to, dirs=ALL):
@@ -153,8 +153,7 @@
 
     pl.semaphore_wait(barrier, sum(h.astype(jnp.int32) for h in has))
     start(edge_copy)
-    for h in range(CHUNKS):
-        send(0, h)
+    send(0, 0)
 
     for d in range(4):
         @pl.when(jnp.logical_not(has[d]))
@@ -174,6 +173,9 @@
         diag[part, :] = tall_diag
         inv_diag[part, :] = 1.0 / tall_diag
         bond_low[part, :] = upright(bond_row[:, j * margin:(j + 1) * margin])
+    sent(edge_copy)
+    for h in range(1, CHUNKS):
+        send(0, h)
     node = lax.broadcasted_iota(jnp.int32, (nodes, margin), 0).astype(F32)
     bonds = bond_low[...]
     bond_high[...] = jnp.where(node == float(nodes - 1), 0.0, pltpu.roll(bonds, nodes - 1, 0))
@@ -227,7 +229,6 @@
         own_part[h] = apply_stacked(own_tile, pair(coarse_out[0, h]))
 
     arrive(edge_copy)
-    sent(edge_copy)
     scale = CHEB_FIRST * CHEB_SECOND * COUPLE_WEIGHT
     keep_stacked(tiles, jnp.concatenate([
         scale * dot_nt(edge_cols[:, d * margin:(d + 1) * margin], edge_in[d].astype(BF16)) for d in range(4)], axis=1))
@@ -254,10 +255,10 @@
         for d in range(4):
             margin_out[t, h, 1, d] = margin_out[t, h, 0, d] + taken[d * margin:(d + 1) * margin]
         parts = take(t, h, 0, 0)
-        for k, dirs in enumerate((SUB, GRP)):
-            taken = fold(dot(cross[block(k), :side], parts))
+        for dirs in ((0,), (1,), GRP):
+            taken = fold(dot(cross[pl.ds(dirs[0] * margin, len(dirs) * margin), :side], parts))
             for d in dirs:
-                margin_out[t, h, 1, d] = margin_out[t, h, 1, d] + taken[(d % 2) * margin:(d % 2 + 1) * margin]
+                margin_out[t, h, 1, d] = margin_out[t, h, 1, d] + taken[(d - dirs[0]) * margin:(d - dirs[0] + 1) * margin]
             send(3 * t + 2, h, dirs)
 
     def add_up(t, h):
@@ -317,8 +318,7 @@
                     parts_out[...] = parts
 
     for h in range(CHUNKS):
-        for k in (3 * ITERS - 2, 3 * ITERS - 1):
-            sent(step_copy(k, h))
+        sent(step_copy(3 * ITERS - 1, h))
 
 
 def put_out(sol_in, head, tail, spread, parts, sol_out, res_out, last, sem):

time: 41.2 us -> 40.5 us (0.983)
  Pallas kernels: 40.3 us -> 39.6 us
    pallas_call x1, Pallas kernels: 39.2 us -> 38.4 us  [per_device(): pl.pallas_call(functools.partial(kernel, mesh.shape['sub'], mesh.shape['g...]
where the time goes in v3:
time: 40.5 us; the launch traced here: 40.3 us
  Pallas kernels  39.6 us (98%)
  between operations  0.64 us (2%)
    pallas_call x1, Pallas kernels, per_device(): pl.pallas_call(functools.partial(kernel, mesh.shape['sub'], mesh.shape['g...  38.4 us
    pallas_call x1, Pallas kernels, per_device(): pl.pallas_call(put_out, out_shape=(jax.ShapeDtypeStruct((nodes, columns),...  1.18 us

profile of v3, /device:TPU:19, one launch (start us, length us, event | category | flops | bytes accessed | tf_op | source)
XLA Modules:
  0.0 40.3 jit_solution(13150942074057547194)
XLA Ops:
  0.6 38.4 %shard_map.86 = (f32[1024,256]{1,0:T(8,128)S(1)}, bf16[1024,128]{1,0:T(8,128)(2,1)S(1)}, f32[1024,128]{1,0:T(8,128)S(1)}, bf16[1024,576]{1,0:T(8,128)(2,1)S(1)}, bf16[256,256]{1,0:T(8,128)(2,1)S(1)}) custom-call(bf16[1024,256]{1,0:T(8,128)(2,1)} %bitcast.12, bf16[1024,1024]{1,0:T(8,128)(2,1)} %bitcast.11, f32[1,1024]{1,0:T(1,128)} %bitcast.14, ...), custom_call_target="tpu_custom_call" | custom-call | tf_op jit(solution)/shard_map/pallas_call | solution.py:382
  39.1 1.2 %shard_map.87 = (f32[1024,256]{1,0:T(8,128)}, bf16[1024,256]{1,0:T(8,128)(2,1)}) custom-call(f32[1024,256]{1,0:T(8,128)S(1)} %get-tuple-element.9.sol_in, bf16[1024,128]{1,0:T(8,128)(2,1)S(1)} %get-tuple-element.10.head, f32[1024,128]{1,0:T(8,128)S(1)} %get-tuple-element.11.tail, bf16[1024,576]{1,0:T(8,128)(2,1)S(1)} %get-tuple-element.12.spread, ...), custom_call_target="tpu_custom_call" | custom-call | tf_op jit(solution)/shard_map/pallas_call | solution.py:393

commit v4 on v3

--- a/solution.py
+++ b/solution.py
@@ -57,7 +57,7 @@
     diag, inv_diag, bond_low, bond_high,
     resid, corr, total, own_part, pulled, came,
     edge_out, edge_in, coarse_out, coarse_in, margin_out, margin_in,
-    edge_recv, send_sem, recv_sem,
+    load_sem, edge_recv, send_sem, recv_sem,
 ):
     nodes, columns = rhs.shape
     defl = basis_t.shape[0]
@@ -68,7 +68,7 @@
     has = [s > 0, s < subs - 1, g > 0, g < groups - 1]
     near = [(s - 1, g), (s + 1, g), (s, g - 1), (s, g + 1)]
 
-    rhs_load = pltpu.make_async_copy(rhs_hbm, rhs, send_sem.at[1, 1, 0])
+    rhs_load = pltpu.make_async_copy(rhs_hbm, rhs, send_sem.at[0, 0])
     rhs_load.start()
 
     barrier = pltpu.get_barrier_semaphore()
@@ -80,19 +80,19 @@
     def edge_copy(d):
         return pltpu.make_async_remote_copy(
             src_ref=edge_out.at[d], dst_ref=edge_in.at[d ^ 1],
-            send_sem=send_sem.at[0, 1, d], recv_sem=edge_recv.at[d ^ 1],
+            send_sem=send_sem.at[1, d], recv_sem=edge_recv.at[d ^ 1],
             device_id=near[d], device_id_type=MESH)
 
     def coarse_copy(t, h, d):
         return pltpu.make_async_remote_copy(
             src_ref=coarse_out.at[t, h], dst_ref=coarse_in.at[t, h, d ^ 1],
-            send_sem=send_sem.at[h, 0, d], recv_sem=recv_sem.at[h, 3 * t % 2, d ^ 1],
+            send_sem=send_sem.at[h, d], recv_sem=recv_sem.at[h, 3 * t % 2, d ^ 1],
             device_id=near[d], device_id_type=MESH)
 
     def margin_copy(t, h, p, d):
         return pltpu.make_async_remote_copy(
             src_ref=margin_out.at[t, h, p, d], dst_ref=margin_in.at[t, h, p, d ^ 1],
-            send_sem=send_sem.at[h, 0, d], recv_sem=recv_sem.at[h, (3 * t + 1 + p) % 2, d ^ 1],
+            send_sem=send_sem.at[h, d], recv_sem=recv_sem.at[h, (3 * t + 1 + p) % 2, d ^ 1],
             device_id=near[d], device_id_type=MESH)
 
     def step_copy(k, h):
@@ -145,7 +145,7 @@
     for d in range(4):
         edge_out[d] = edges[:, d * margin:(d + 1) * margin]
     rhs_load.wait()
-    load = pltpu.make_async_copy(inverse_hbm, inverse, send_sem.at[1, 1, 1])
+    load = pltpu.make_async_copy(inverse_hbm, inverse, load_sem)
     load.start()
     first = dot(basis_t[...], rhs[...])
     for h in range(CHUNKS):
@@ -368,8 +368,9 @@
         pltpu.VMEM((ITERS, CHUNKS, 4, defl, width), F32),
         pltpu.VMEM((ITERS, CHUNKS, 2, 4, margin, width), F32),
         pltpu.VMEM((ITERS, CHUNKS, 2, 4, margin, width), F32),
+        pltpu.SemaphoreType.DMA,
         pltpu.SemaphoreType.DMA((4,)),
-        pltpu.SemaphoreType.DMA((CHUNKS, 2, 4)),
+        pltpu.SemaphoreType.DMA((CHUNKS, 4)),
         pltpu.SemaphoreType.DMA((CHUNKS, 2, 4)),
     ]
     results = (

time: 40.5 us -> 40.4 us (level)
  no operation moved by 1% of the time
where the time goes in v4:
time: 40.4 us; the launch traced here: 40.2 us
  Pallas kernels  39.6 us (98%)
  between operations  0.64 us (2%)
    pallas_call x1, Pallas kernels, per_device(): pl.pallas_call(functools.partial(kernel, mesh.shape['sub'], mesh.shape['g...  38.4 us
    pallas_call x1, Pallas kernels, per_device(): pl.pallas_call(put_out, out_shape=(jax.ShapeDtypeStruct((nodes, columns),...  1.18 us

profile of v4, /device:TPU:19, one launch (start us, length us, event | category | flops | bytes accessed | tf_op | source)
XLA Modules:
  0.0 40.2 jit_solution(7325827058683300624)
XLA Ops:
  0.6 38.4 %shard_map.86 = (f32[1024,256]{1,0:T(8,128)S(1)}, bf16[1024,128]{1,0:T(8,128)(2,1)S(1)}, f32[1024,128]{1,0:T(8,128)S(1)}, bf16[1024,576]{1,0:T(8,128)(2,1)S(1)}, bf16[256,256]{1,0:T(8,128)(2,1)S(1)}) custom-call(bf16[1024,256]{1,0:T(8,128)(2,1)} %bitcast.12, bf16[1024,1024]{1,0:T(8,128)(2,1)} %bitcast.11, f32[1,1024]{1,0:T(1,128)} %bitcast.14, ...), custom_call_target="tpu_custom_call" | custom-call | tf_op jit(solution)/shard_map/pallas_call | solution.py:383
  39.0 1.2 %shard_map.87 = (f32[1024,256]{1,0:T(8,128)}, bf16[1024,256]{1,0:T(8,128)(2,1)}) custom-call(f32[1024,256]{1,0:T(8,128)S(1)} %get-tuple-element.9.sol_in, bf16[1024,128]{1,0:T(8,128)(2,1)S(1)} %get-tuple-element.10.head, f32[1024,128]{1,0:T(8,128)S(1)} %get-tuple-element.11.tail, bf16[1024,576]{1,0:T(8,128)(2,1)S(1)} %get-tuple-element.12.spread, ...), custom_call_target="tpu_custom_call" | custom-call | tf_op jit(solution)/shard_map/pallas_call | solution.py:394
